TPU v7x, 32 devices: a whole 2x2x4 slice. The times are simulated.
32 devices in a mesh: dp: 8 (over z, y), tensor: 4 (over x, core).
Axes of the slice: x: 2, y: 2, z: 4, core: 2. Of those that a mesh axis runs over, the one named last changes fastest.
Arguments:
- inputs: bfloat16 [4096, 512], P('dp'), may hold values from -6 to 6
- query_weight: bfloat16 [512, 512], P(None, 'tensor'), may hold values from -0.25 to 0.25
- key_weight: bfloat16 [512, 512], P(None, 'tensor'), may hold values from -0.25 to 0.25
- value_weight: bfloat16 [512, 512], P(None, 'tensor'), may hold values from -0.25 to 0.25
- query_bias: float32 [512], P('tensor'), may hold values from -3 to 3
- value_bias: float32 [512], P('tensor'), may hold values from -3 to 3
- position_bias: float32 [49, 16], P(None, 'tensor'), may hold values from -4 to 4
- proj_weight: bfloat16 [512, 512], P('tensor'), may hold values from -0.5 to 0.5
- proj_bias: float32 [512], replicated, may hold values from -2 to 2
- norm1_gain: float32 [512], replicated, may hold values from 0.5 to 1.5
- norm1_shift: float32 [512], replicated, may hold values from -2 to 2
- norm2_gain: float32 [512], replicated, may hold values from 0.5 to 1.5
- norm2_shift: float32 [512], replicated, may hold values from -2 to 2
- up_weight: bfloat16 [512, 2048], P(None, 'tensor'), may hold values from -0.25 to 0.25
- up_bias: float32 [2048], P('tensor'), may hold values from -2 to 2
- down_weight: bfloat16 [2048, 512], P('tensor'), may hold values from -0.25 to 0.25
- down_bias: float32 [512], replicated, may hold values from -2 to 2
- segment_ids: int32 [8, 512], P('dp'), may hold values from 0 to 3, never falling along the last dimension, each value on 1 to 256 neighbouring positions
- valid_mask: int32 [8, 512], P('dp'), may hold values 0 or 1
- position_index: int32 [16, 16], replicated, may hold values from 0 to 48
- out_cotangent: bfloat16 [4096, 512], P('dp'), may hold values from -6 to 6
Outputs:
- layer_out: float32 [4096, 512], P('dp')
- input_grad: float32 [4096, 512], P('dp')
- query_weight_grad: float32 [512, 512], P(None, 'tensor')
- key_weight_grad: float32 [512, 512], P(None, 'tensor')
- value_weight_grad: float32 [512, 512], P(None, 'tensor')
- query_bias_grad: float32 [512], P('tensor')
- value_bias_grad: float32 [512], P('tensor')
- position_bias_grad: float32 [49, 16], P(None, 'tensor')
- proj_weight_grad: float32 [512, 512], P('tensor')
- proj_bias_grad: float32 [512], replicated
- norm1_gain_grad: float32 [512], replicated
- norm1_shift_grad: float32 [512], replicated
- norm2_gain_grad: float32 [512], replicated
- norm2_shift_grad: float32 [512], replicated
- up_weight_grad: float32 [512, 2048], P(None, 'tensor')
- up_bias_grad: float32 [2048], P('tensor')
- down_weight_grad: float32 [2048, 512], P('tensor')
- down_bias_grad: float32 [512], replicated
Inputs may be any that keep to these rules, and one draw needn't show every extreme that they name: `segment_ids`: within each grid the clip numbers never fall, and each clip has 1 to 256 patches.
All inputs are finite; a program needn't handle non-finite values. No bound on the sum of `valid_mask` on one device may be relied on, other than what follows from the above.
Results may differ from a plain program's by a relative error of at most 0.012.
Values may be sent and summed in bfloat16 or wider, within the bound.
No kernel may reach another device: no remote copies, remote signals or barrier semaphores. Data moves between devices by JAX's collectives and lax.ppermute only.
A program may use at most 64 MiB of HBM per device.

v0:
```python
import jax
import jax.numpy as jnp
from jax import lax
from jax.sharding import PartitionSpec as P

HD = 32
GH = 64
GW = 8
WS = 4
NEG_FILL = -1e30


def normalize(value):
    centre = value - jnp.mean(value, axis=-1, keepdims=True)
    spread = jnp.mean(centre * centre, axis=-1, keepdims=True)
    inverse = lax.rsqrt(spread + 1e-06)
    return (centre * inverse, inverse)


def norm_back(grad_out, normed, inverse, gain):
    scaled = grad_out * gain
    first_mean = jnp.mean(scaled, axis=-1, keepdims=True)
    second_mean = jnp.mean(scaled * normed, axis=-1, keepdims=True)
    return inverse * (scaled - first_mean - normed * second_mean)


def to_windows(field):
    grids = field.shape[0] // (GH * GW)
    chans = field.shape[-1]
    shaped = field.reshape(grids, GH // WS, WS, GW // WS, WS, chans)
    return shaped.transpose(0, 1, 3, 2, 4, 5).reshape(-1, WS * WS, chans)


def from_windows(field):
    chans = field.shape[-1]
    grids = field.shape[0] // (GH // WS * (GW // WS))
    shaped = field.reshape(grids, GH // WS, GW // WS, WS, WS, chans)
    return shaped.transpose(0, 1, 3, 2, 4, 5).reshape(-1, chans)


def matmul(left, right):
    return jnp.dot(left, right, preferred_element_type=jnp.float32)


def gelu_fn(value):
    return jax.nn.gelu(value, approximate=True)


def tensor_reduce(col_grads, row_grads, small_grads):
    return (col_grads, row_grads, small_grads)


def shards(
    inputs,
    query_weight,
    key_weight,
    value_weight,
    query_bias,
    value_bias,
    position_bias,
    proj_weight,
    proj_bias,
    norm1_gain,
    norm1_shift,
    norm2_gain,
    norm2_shift,
    up_weight,
    up_bias,
    down_weight,
    down_bias,
    segment_ids,
    valid_mask,
    position_index,
    out_cotangent,
):
    window = WS * WS
    factor = HD ** (-0.5)
    width = inputs.shape[1]
    x_rows = to_windows(inputs).reshape(-1, width)
    cot_rows = to_windows(out_cotangent).reshape(-1, width)
    seg_rows = to_windows(segment_ids.reshape(-1, 1)).reshape(-1)
    valid_rows = to_windows(valid_mask.reshape(-1, 1)).reshape(-1)
    wq, wk, wv, w_up = (query_weight, key_weight, value_weight, up_weight)
    w_proj, w_down = (proj_weight, down_weight)
    b_query, b_value, b_up, rel_bias = (query_bias, value_bias, up_bias, position_bias)
    local_heads = wq.shape[1] // HD
    xfull = x_rows.astype(jnp.float32)
    normed1, inverse1 = normalize(xfull)
    first = (normed1 * norm1_gain + norm1_shift).astype(jnp.bfloat16)
    query = (matmul(first, wq) + b_query).astype(jnp.bfloat16)
    key = matmul(first, wk).astype(jnp.bfloat16)
    value = (matmul(first, wv) + b_value).astype(jnp.bfloat16)
    qwin = query.reshape(-1, window, local_heads, HD)
    kwin = key.reshape(-1, window, local_heads, HD)
    vwin = value.reshape(-1, window, local_heads, HD)
    offsets = lax.broadcasted_iota(jnp.int32, (window * window, rel_bias.shape[0]), 1)
    onehot = (position_index.reshape(-1, 1) == offsets).astype(jnp.float32)
    bias = jnp.dot(onehot, rel_bias, precision=lax.Precision.HIGHEST)
    bias = bias.reshape(window, window, local_heads).transpose(2, 0, 1)
    segwin = seg_rows.reshape(-1, window)
    validwin = valid_rows.reshape(-1, window)
    selfs = jnp.eye(window, dtype=jnp.int32) > 0
    allowed = (segwin[:, :, None] == segwin[:, None, :]) & (
        (validwin[:, None, :] > 0) | selfs[None]
    )
    scores = (
        jnp.einsum("wqhd,wkhd->whqk", qwin, kwin, preferred_element_type=jnp.float32) * factor
        + bias[None]
    )
    scores = jnp.where(allowed[:, None], scores, NEG_FILL)
    top = jnp.max(scores, axis=-1, keepdims=True)
    expo = jnp.exp(scores - top)
    probs = expo / jnp.sum(expo, axis=-1, keepdims=True)
    probs_low = probs.astype(jnp.bfloat16)
    attended = jnp.einsum("whqk,wkhd->wqhd", probs_low, vwin, preferred_element_type=jnp.float32)
    attended = attended.reshape(-1, local_heads * HD).astype(jnp.bfloat16)
    attn_out = lax.psum(matmul(attended, w_proj), "tensor")
    mid = xfull + attn_out + proj_bias
    normed2, inverse2 = normalize(mid)
    second = (normed2 * norm2_gain + norm2_shift).astype(jnp.bfloat16)
    pre = matmul(second, w_up) + b_up
    hidden_full, gelu_pull = jax.vjp(gelu_fn, pre)
    hidden = hidden_full.astype(jnp.bfloat16)
    mlp_out = lax.psum(matmul(hidden, w_down).astype(jnp.bfloat16), "tensor").astype(jnp.float32)
    layer_rows = mid + mlp_out + down_bias
    grad_out = cot_rows.astype(jnp.float32)
    down_bias_grad = jnp.sum(grad_out, axis=0)
    grad_mlp = grad_out.astype(jnp.bfloat16)
    down_weight_grad = matmul(hidden.T, grad_mlp)
    grad_hidden = matmul(grad_mlp, w_down.T)
    grad_pre = gelu_pull(grad_hidden)[0].astype(jnp.bfloat16)
    up_bias_grad = jnp.sum(grad_pre.astype(jnp.float32), axis=0)
    up_weight_grad = matmul(second.T, grad_pre)
    grad_second = lax.psum(matmul(grad_pre, w_up.T), "tensor")
    norm2_gain_grad = jnp.sum(grad_second * normed2, axis=0)
    norm2_shift_grad = jnp.sum(grad_second, axis=0)
    grad_mid = grad_out + norm_back(grad_second, normed2, inverse2, norm2_gain)
    proj_bias_grad = jnp.sum(grad_mid, axis=0)
    grad_proj = grad_mid.astype(jnp.bfloat16)
    proj_weight_grad = matmul(attended.T, grad_proj)
    grad_att = matmul(grad_proj, w_proj.T).astype(jnp.bfloat16)
    gwin = grad_att.reshape(-1, window, local_heads, HD)
    grad_probs = jnp.einsum("wqhd,wkhd->whqk", gwin, vwin, preferred_element_type=jnp.float32)
    grad_value = jnp.einsum(
        "whqk,wqhd->wkhd", probs_low, gwin, preferred_element_type=jnp.float32
    ).astype(jnp.bfloat16)
    grad_scores = probs * (grad_probs - jnp.sum(probs * grad_probs, axis=-1, keepdims=True))
    grad_scores = grad_scores.astype(jnp.bfloat16)
    grad_query = (
        factor
        * jnp.einsum("whqk,wkhd->wqhd", grad_scores, kwin, preferred_element_type=jnp.float32)
    ).astype(jnp.bfloat16)
    grad_key = (
        factor
        * jnp.einsum("whqk,wqhd->wkhd", grad_scores, qwin, preferred_element_type=jnp.float32)
    ).astype(jnp.bfloat16)
    score_total = jnp.sum(grad_scores.astype(jnp.float32), axis=0)
    score_total = score_total.transpose(1, 2, 0).reshape(window * window, local_heads)
    position_bias_grad = jnp.dot(onehot.T, score_total, precision=lax.Precision.HIGHEST)
    query_rows = grad_query.reshape(-1, local_heads * HD)
    key_rows = grad_key.reshape(-1, local_heads * HD)
    value_rows = grad_value.reshape(-1, local_heads * HD)
    query_bias_grad = jnp.sum(query_rows.astype(jnp.float32), axis=0)
    value_bias_grad = jnp.sum(value_rows.astype(jnp.float32), axis=0)
    query_weight_grad = matmul(first.T, query_rows)
    key_weight_grad = matmul(first.T, key_rows)
    value_weight_grad = matmul(first.T, value_rows)
    first_part = matmul(query_rows, wq.T) + matmul(key_rows, wk.T) + matmul(value_rows, wv.T)
    grad_first = lax.psum(first_part, "tensor")
    norm1_gain_grad = jnp.sum(grad_first * normed1, axis=0)
    norm1_shift_grad = jnp.sum(grad_first, axis=0)
    grad_rows_out = grad_mid + norm_back(grad_first, normed1, inverse1, norm1_gain)
    (
        (wq_part, wk_part, wv_part, rel_part, w1_part),
        (bq_part, bv_part, wo_part, b1_part, w2_part),
        (bo_part, g1_part, s1_part, b2_part, g2_part, s2_part),
    ) = tensor_reduce(
        (query_weight_grad, key_weight_grad, value_weight_grad, position_bias_grad, up_weight_grad),
        (query_bias_grad, value_bias_grad, proj_weight_grad, up_bias_grad, down_weight_grad),
        (
            proj_bias_grad,
            norm1_gain_grad,
            norm1_shift_grad,
            down_bias_grad,
            norm2_gain_grad,
            norm2_shift_grad,
        ),
    )
    every = lax.psum(
        (
            wq_part,
            wk_part,
            wv_part,
            bq_part,
            bv_part,
            rel_part,
            wo_part,
            bo_part,
            g1_part,
            s1_part,
            w1_part,
            b1_part,
            w2_part,
            b2_part,
            g2_part,
            s2_part,
        ),
        "dp",
    )
    early_set = every[:10]
    late_set = every[10:]
    layer_out = from_windows(layer_rows.reshape(-1, window, width))
    input_grad = from_windows(grad_rows_out.reshape(-1, window, width))
    (
        wq_total,
        wk_total,
        wv_total,
        bq_total,
        bv_total,
        rel_total,
        wo_total,
        bo_total,
        g1_total,
        s1_total,
    ) = early_set
    w1_total, b1_total, w2_total, b2_total, g2_total, s2_total = late_set
    return (
        layer_out,
        input_grad,
        wq_total,
        wk_total,
        wv_total,
        bq_total,
        bv_total,
        rel_total,
        wo_total,
        bo_total,
        g1_total,
        s1_total,
        g2_total,
        s2_total,
        w1_total,
        b1_total,
        w2_total,
        b2_total,
    )


def solution(mesh):
    return jax.shard_map(
        shards,
        mesh=mesh,
        in_specs=(
            P("dp", None),
            P(None, "tensor"),
            P(None, "tensor"),
            P(None, "tensor"),
            P("tensor"),
            P("tensor"),
            P(None, "tensor"),
            P("tensor", None),
            P(),
            P(),
            P(),
            P(),
            P(),
            P(None, "tensor"),
            P("tensor"),
            P("tensor", None),
            P(),
            P("dp", None),
            P("dp", None),
            P(),
            P("dp", None),
        ),
        out_specs=(
            P("dp", None),
            P("dp", None),
            P(None, "tensor"),
            P(None, "tensor"),
            P(None, "tensor"),
            P("tensor"),
            P("tensor"),
            P(None, "tensor"),
            P("tensor", None),
            P(),
            P(),
            P(),
            P(),
            P(),
            P(None, "tensor"),
            P("tensor"),
            P("tensor", None),
            P(),
        ),
        check_vma=False,
    )
```

profile of v0, /device:TPU:0, one launch (start us, length us, event | category | flops | bytes accessed | tf_op | source)
XLA Modules:
  0.0 360.2 jit_solution(3782836094382820206)
XLA Ops:
  7.8 1.4 reshape.268
  15.8 1.6 reshape.266
  20.2 2.0 reshape.254
  22.2 1.6 fusion.12
  26.8 2.8 fusion.44
  29.6 1.8 fusion.9
  39.8 1.4 fusion.50
  41.3 31.5 %all-reduce.8.cloned.1.call-done = f32[512,512]{1,0:T(8,128)} async-done(((f32[512,512]{1,0:T(8,128)}), f32[512,512]{1,0:T(8,128)}) %all-reduce.8.cloned.1.call-update) | async-done | bytes 1048592 | tf_op jit(solution)/shard_map/psum | solution.py:117
  72.7 1.4 fusion.43
  75.4 1.7 convert_reduce_fusion.1
  77.2 1.6 fusion.38
  78.7 1.4 fusion.51
  80.2 2.7 convolution_convert_fusion.1
  82.9 2.7 fusion.40
  85.9 30.9 %all-reduce.12.cloned.1.call-done = f32[512,512]{1,0:T(8,128)} async-done(((f32[512,512]{1,0:T(8,128)}), f32[512,512]{1,0:T(8,128)}) %all-reduce.12.cloned.1.call-update) | async-done | bytes 1048592 | tf_op jit(solution)/shard_map/psum | solution.py:134
  116.8 1.7 multiply_reduce_fusion
  118.6 34.2 %all-reduce.10.cloned.1.call-done = bf16[512,512]{1,0:T(8,128)(2,1)} async-done(((bf16[512,512]{1,0:T(8,128)(2,1)}), bf16[512,512]{1,0:T(8,128)(2,1)}) %all-reduce.10.cloned.1.call-update) | async-done | bytes 524304 | tf_op jit(solution)/shard_map/psum | solution.py:124
  152.8 3.0 fusion.42
  158.1 2.9 convert_reduce_fusion.3
  170.1 1.3 convolution_add_fusion
  176.6 2.5 reshape_reshape.15
  179.2 2.3 copy.105
  181.5 2.6 reshape.258
  184.3 23.4 %all-reduce.14.cloned.1.call-done = f32[512,512]{1,0:T(8,128)} async-done(((f32[512,512]{1,0:T(8,128)}), f32[512,512]{1,0:T(8,128)}) %all-reduce.14.cloned.1.call-update) | async-done | bytes 1048592 | tf_op jit(solution)/shard_map/psum | solution.py:169
  207.8 1.8 multiply_reduce_fusion.1
  209.6 1.3 multiply_add_fusion
  211.0 1.5 reshape_reshape.17
  212.6 1.3 reshape.264
  214.6 39.6 %all-reduce = (f32[128]{0:T(128)}, f32[128]{0:T(128)}, f32[49,4]{0,1:T(4,128)}, f32[512]{0:T(512)}, f32[512]{0:T(512)}, /*index=5*/f32[512]{0:T(512)}, f32[512]{...) all-reduce(f32[128]{0:T(128)S(1)} %reduce_sum.195, ...), channel_id=1, replica_groups=mesh['dp'=8,'tensor'=4] {'dp'}, use_global_device_ids=true, to_apply=%region_19.20 | all-reduce | flops 4036 | bytes 32288 | tf_op jit(solution)/shard_map/psum | solution.py:189
  254.2 91.6 %all-reduce.16.cloned.1.call-done = (f32[512,128]{1,0:T(8,128)}, f32[512,128]{1,0:T(8,128)}, f32[512,128]{1,0:T(8,128)}, f32[128,512]{1,0:T(8,128)}, f32[512,512]{1,0:T(8,128)}, /*index=5*/f32[512,512]{1,0:T(8,128)}) async-done(((f32[512,128]{1,0:T(8,128)}, f32[512,128]{1,0:T(8,128)}, f32[512,128]{1,0:T(8,128)}, f32[128,512]{1,0:T(8,128)}, f32[512,512]{1,0:T(8,128)}, /*index=5*/f32[512,512]{1,0:T(8,128)}), ...) | async-done | bytes 3145744 | tf_op jit(solution)/shard_map/psum | solution.py:189
  345.9 1.8 copy.170
  347.6 1.7 copy.171
  (196 shorter events, 44.6 us)
Async XLA Ops:
  7.2 67.3 %copy-start = (bf16[512,512]{1,0:T(8,128)(2,1)S(1)}, bf16[512,512]{1,0:T(8,128)(2,1)}, u32[]{:S(2)}) copy-start(bf16[512,512]{1,0:T(8,128)(2,1)} %param.34) | copy-start | bytes 1572868
  7.2 65.5 %all-reduce.8.cloned.1.call-start = ((), (), s32[]{:S(2)}) async-start(), calls=%async_computation | async-start | bytes 2097152 | tf_op jit(solution)/shard_map/psum | solution.py:117
  9.6 7.8 %copy-start.33 = (f32[512]{0:T(512)}, f32[512]{0:T(512)S(1)}, u32[]{:S(2)}) copy-start(f32[512]{0:T(512)S(1)} %div.35) | copy-start | bytes 6148
  13.5 1.2 copy-start.51
  15.8 1.6 copy-start.35
  15.8 1.6 copy-start.31
  15.8 1.6 copy-start.40
  20.2 2.0 copy-start.19
  25.0 4.6 %copy-start.8 = (bf16[32,16,4,32]{3,2,1,0:T(4,128)(2,1)}, bf16[32,16,4,32]{3,2,1,0:T(4,128)(2,1)S(1)}, u32[]{:S(2)}) copy-start(bf16[32,16,4,32]{3,2,1,0:T(4,128)(2,1)S(1)} %reshape.255) | copy-start | bytes 393220
  29.6 1.8 copy-start.29
  33.8 83.0 %all-reduce.12.cloned.1.call-start = ((), (), s32[]{:S(2)}) async-start(), calls=%async_computation.2 | async-start | bytes 2097152 | tf_op jit(solution)/shard_map/psum | solution.py:134
  37.3 2.5 copy-start.5
  38.6 1.2 copy-start.25
  39.8 32.9 %copy-start.44 = (f32[512]{0:T(512)S(1)}, f32[512]{0:T(512)}, u32[]{:S(2)}) copy-start(f32[512]{0:T(512)} %param.29) | copy-start | bytes 6148
  75.4 1.8 copy-start.6
  77.1 1.6 copy-start.57
  77.2 1.6 copy-start.10
  80.2 72.6 %all-reduce.10.cloned.1.call-start = ((), (), s32[]{:S(2)}) async-start(), calls=%async_computation.1 | async-start | bytes 1048576 | tf_op jit(solution)/shard_map/psum | solution.py:124
  85.7 122.1 %all-reduce.14.cloned.1.call-start = ((), (), s32[]{:S(2)}) async-start(), calls=%async_computation.3 | async-start | bytes 2097152 | tf_op jit(solution)/shard_map/psum | solution.py:169
  118.6 34.2 %copy-start.46 = (f32[512]{0:T(512)S(1)}, f32[512]{0:T(512)}, u32[]{:S(2)}) copy-start(f32[512]{0:T(512)} %param.37) | copy-start | bytes 6148
  155.8 2.3 copy-start.11
  158.1 2.9 copy-start.17
  158.1 2.9 copy-start.18
  171.5 2.1 copy-start.2
  171.5 174.4 %all-reduce.16.cloned.1.call-start = ((), (), s32[]{:S(2)}) async-start(), calls=%async_computation.4 | async-start | bytes 6291456 | tf_op jit(solution)/shard_map/psum | solution.py:189
  181.5 2.6 copy-start.53
  184.1 23.7 %copy-start.34 = (f32[512]{0:T(512)S(1)}, f32[512]{0:T(512)}, u32[]{:S(2)}) copy-start(f32[512]{0:T(512)} %copy-done.33) | copy-start | bytes 6148
  184.1 23.7 %copy-start.36 = (f32[512]{0:T(512)S(1)}, f32[512]{0:T(512)}, u32[]{:S(2)}) copy-start(f32[512]{0:T(512)} %copy-done.35) | copy-start | bytes 6148
  207.8 1.8 copy-start.7
  345.9 3.4 copy-start.27
  345.9 5.2 %copy-start.13 = (f32[512,512]{1,0:T(8,128)S(1)}, f32[512,512]{1,0:T(8,128)}, u32[]{:S(2)}) copy-start(f32[512,512]{1,0:T(8,128)} %get-tuple-element.76) | copy-start | bytes 3145732
  351.1 1.6 copy-start.12
  (31 other events, 30.0 us)
Sparse Core Ops, SparseCore 0:
  33.9 38.7 all-reduce.7
  80.3 36.4 all-reduce.11
  119.2 33.5 all-reduce.9
  171.6 36.1 all-reduce.13
  213.6 132.1 all-reduce.15
where the time goes:
time: 362 us; the launch traced here: 360 us
  waiting for transfers between devices  212 us (59%)
  local copies, waits for them, and re-layouts  47.8 us (13%)
  blocking collectives  39.6 us (11%)
  matrix products  31.7 us (9%)
  other arithmetic  14.5 us (4%)
  between operations  14.4 us (4%)
    psum x1, waiting for transfers between devices, shards(): lax.psum((wq_part, wk_part, wv_part, bq_part, bv_part, rel_part, wo_part,...  91.6 us
    psum x1, blocking collectives, shards(): lax.psum((wq_part, wk_part, wv_part, bq_part, bv_part, rel_part, wo_part,...  39.6 us
    psum x1, waiting for transfers between devices, shards(): lax.psum(matmul(hidden, w_down).astype(jnp.bfloat16), 'tensor')  34.2 us
    psum x1, waiting for transfers between devices, shards(): attn_out = lax.psum(matmul(attended, w_proj), 'tensor')  31.5 us
    psum x1, waiting for transfers between devices, shards(): grad_second = lax.psum(matmul(grad_pre, w_up.T), 'tensor')  30.9 us
    psum x1, waiting for transfers between devices, shards(): grad_first = lax.psum(first_part, 'tensor')  23.4 us
    dot_general x18, matrix products, matmul(): return jnp.dot(left, right, preferred_element_type=jnp.float32)  22 us
    unnamed x123, local copies, waits for them, and re-layouts  17.8 us
  transfers between devices with their start and end apart: 5, of which 5 were waited for; matrix products, arithmetic and copies ran while one was open for 9% of the time, Pallas kernels for 0%

commit v1 on v0

--- a/solution.py
+++ b/solution.py
@@ -121,7 +121,9 @@
     pre = matmul(second, w_up) + b_up
     hidden_full, gelu_pull = jax.vjp(gelu_fn, pre)
     hidden = hidden_full.astype(jnp.bfloat16)
-    mlp_out = lax.psum(matmul(hidden, w_down).astype(jnp.bfloat16), "tensor").astype(jnp.float32)
+    mlp_out = jnp.sum(
+        lax.all_gather(matmul(hidden, w_down).astype(jnp.bfloat16), "tensor"), axis=0
+    ).astype(jnp.float32)
     layer_rows = mid + mlp_out + down_bias
     grad_out = cot_rows.astype(jnp.float32)
     down_bias_grad = jnp.sum(grad_out, axis=0)

time: 362 us -> 354 us (0.978)
  waiting for transfers between devices: 212 us -> 198 us
  matrix products: 31.7 us -> 37.6 us
  local copies, waits for them, and re-layouts: 47.8 us -> 43 us
  other arithmetic: 14.5 us -> 19 us
    psum x1 -> x0, waiting for transfers between devices: 34.2 us -> none  [shards(): lax.psum(matmul(hidden, w_down).astype(jnp.bfloat16), 'tensor')]
    all_gather x0 -> x1, waiting for transfers between devices: none -> 22.8 us  [shards(): lax.all_gather(matmul(hidden, w_down).astype(jnp.bfloat16), 'tensor')]
    unnamed x123 -> x107, local copies, waits for them, and re-layouts: 17.8 us -> 11.7 us
    dot_general x18, matrix products: 22 us -> 26.9 us  [matmul(): return jnp.dot(left, right, preferred_element_type=jnp.float32)]
    psum x1, waiting for transfers between devices: 30.9 us -> 26.5 us  [shards(): grad_second = lax.psum(matmul(grad_pre, w_up.T), 'tensor')]
  transfers between devices with their start and end apart: 5 -> 5, of which waited for: 5 -> 5; matrix products, arithmetic and copies ran while one was open for 9% -> 10% of each run, Pallas kernels for 0% -> 0%
where the time goes in v1:
time: 354 us; the launch traced here: 352 us
  waiting for transfers between devices  198 us (56%)
  local copies, waits for them, and re-layouts  43 us (12%)
  blocking collectives  39.7 us (11%)
  matrix products  37.6 us (11%)
  other arithmetic  19 us (5%)
  between operations  14.5 us (4%)
    psum x1, waiting for transfers between devices, shards(): lax.psum((wq_part, wk_part, wv_part, bq_part, bv_part, rel_part, wo_part,...  92.4 us
    psum x1, blocking collectives, shards(): lax.psum((wq_part, wk_part, wv_part, bq_part, bv_part, rel_part, wo_part,...  39.7 us
    psum x1, waiting for transfers between devices, shards(): attn_out = lax.psum(matmul(attended, w_proj), 'tensor')  32.1 us
    dot_general x18, matrix products, matmul(): return jnp.dot(left, right, preferred_element_type=jnp.float32)  26.9 us
    psum x1, waiting for transfers between devices, shards(): grad_second = lax.psum(matmul(grad_pre, w_up.T), 'tensor')  26.5 us
    psum x1, waiting for transfers between devices, shards(): grad_first = lax.psum(first_part, 'tensor')  24.4 us
    all_gather x1, waiting for transfers between devices, shards(): lax.all_gather(matmul(hidden, w_down).astype(jnp.bfloat16), 'tensor')  22.8 us
    unnamed x107, local copies, waits for them, and re-layouts  11.7 us
  transfers between devices with their start and end apart: 5, of which 5 were waited for; matrix products, arithmetic and copies ran while one was open for 10% of the time, Pallas kernels for 0%

profile of v1, /device:TPU:0, one launch (start us, length us, event | category | flops | bytes accessed | tf_op | source)
XLA Modules:
  0.0 352.5 jit_solution(9671133157634487677)
XLA Ops:
  16.1 1.6 reshape.266
  20.7 2.0 reshape.254
  22.6 1.6 fusion.12
  27.4 2.8 fusion.44
  30.2 1.8 fusion.9
  36.1 2.0 reshape_reshape.16
  38.1 2.6 fusion.50
  40.7 32.1 %all-reduce.7.cloned.1.call-done = f32[512,512]{1,0:T(8,128)} async-done(((f32[512,512]{1,0:T(8,128)}), f32[512,512]{1,0:T(8,128)}) %all-reduce.7.cloned.1.call-update) | async-done | bytes 1048592 | tf_op jit(solution)/shard_map/psum | solution.py:117
  72.8 1.5 fusion.43
  74.6 2.7 convert_reduce_fusion.1
  79.7 2.5 convolution_convert_fusion.1
  85.0 3.0 fusion.38
  88.0 1.7 fusion.40
  89.7 26.5 %all-reduce.9.cloned.1.call-done = f32[512,512]{1,0:T(8,128)} async-done(((f32[512,512]{1,0:T(8,128)}), f32[512,512]{1,0:T(8,128)}) %all-reduce.9.cloned.1.call-update) | async-done | bytes 1048592 | tf_op jit(solution)/shard_map/psum | solution.py:136
  116.2 1.7 multiply_reduce_fusion
  117.9 22.8 %all-gather.3.cloned.1.call-done = bf16[2048,512]{1,0:T(8,128)(2,1)} async-done(((bf16[512,512]{1,0:T(8,128)(2,1)}), bf16[2048,512]{1,0:T(8,128)(2,1)}) %all-gather.3.cloned.1.call-update) | async-done | bytes 2097168 | tf_op jit(solution)/shard_map/all_gather | solution.py:125
  140.7 2.9 reduce_sum.201
  143.6 3.0 fusion.42
  148.2 3.1 convert_reduce_fusion.3
  153.3 1.7 convert_reduce_fusion.4
  166.7 2.5 reshape_reshape.15
  169.2 2.4 copy.105
  171.6 2.6 reshape.258
  174.4 24.4 %all-reduce.11.cloned.1.call-done = f32[512,512]{1,0:T(8,128)} async-done(((f32[512,512]{1,0:T(8,128)}), f32[512,512]{1,0:T(8,128)}) %all-reduce.11.cloned.1.call-update) | async-done | bytes 1048592 | tf_op jit(solution)/shard_map/psum | solution.py:171
  198.8 1.8 multiply_reduce_fusion.1
  202.0 1.5 reshape_reshape.17
  205.1 39.7 %all-reduce = (f32[128]{0:T(128)}, f32[128]{0:T(128)}, f32[49,4]{0,1:T(4,128)}, f32[512]{0:T(512)}, f32[512]{0:T(512)}, /*index=5*/f32[512]{0:T(512)}, f32[512]{...) all-reduce(f32[128]{0:T(128)S(1)} %reduce_sum.208, ...), channel_id=1, replica_groups=mesh['dp'=8,'tensor'=4] {'dp'}, use_global_device_ids=true, to_apply=%region_19.20 | all-reduce | flops 4036 | bytes 32288 | tf_op jit(solution)/shard_map/psum | solution.py:191
  244.7 92.4 %all-reduce.13.cloned.1.call-done = (f32[512,128]{1,0:T(8,128)}, f32[512,128]{1,0:T(8,128)}, f32[512,128]{1,0:T(8,128)}, f32[128,512]{1,0:T(8,128)}, f32[512,512]{1,0:T(8,128)}, /*index=5*/f32[512,512]{1,0:T(8,128)}) async-done(((f32[512,128]{1,0:T(8,128)}, f32[512,128]{1,0:T(8,128)}, f32[512,128]{1,0:T(8,128)}, f32[128,512]{1,0:T(8,128)}, f32[512,512]{1,0:T(8,128)}, /*index=5*/f32[512,512]{1,0:T(8,128)}), ...) | async-done | bytes 3145744 | tf_op jit(solution)/shard_map/psum | solution.py:191
  337.2 1.8 copy.169
  339.0 1.7 copy.170
  340.7 1.7 copy.171
  342.3 1.7 copy.172
  (181 shorter events, 44.3 us)
Async XLA Ops:
  7.2 67.4 %copy-start = (bf16[512,512]{1,0:T(8,128)(2,1)S(1)}, bf16[512,512]{1,0:T(8,128)(2,1)}, u32[]{:S(2)}) copy-start(bf16[512,512]{1,0:T(8,128)(2,1)} %param.34) | copy-start | bytes 1572868
  7.2 65.6 %all-reduce.7.cloned.1.call-start = ((), (), s32[]{:S(2)}) async-start(), calls=%async_computation | async-start | bytes 2097152 | tf_op jit(solution)/shard_map/psum | solution.py:117
  9.5 4.9 %copy-start.44 = (s32[1,512]{1,0:T(1,128)S(1)}, s32[1,512]{1,0:T(1,128)}, u32[]{:S(2)}) copy-start(s32[1,512]{1,0:T(1,128)} %param.38) | copy-start | bytes 6148
  13.2 5.6 %copy-start.23 = (bf16[512,128]{1,0:T(8,128)(2,1)S(1)}, bf16[512,128]{1,0:T(8,128)(2,1)}, u32[]{:S(2)}) copy-start(bf16[512,128]{1,0:T(8,128)(2,1)} %param.23) | copy-start | bytes 393220
  17.7 4.9 %copy-start.22 = (bf16[512,128]{1,0:T(8,128)(2,1)S(1)}, bf16[512,128]{1,0:T(8,128)(2,1)}, u32[]{:S(2)}) copy-start(bf16[512,128]{1,0:T(8,128)(2,1)} %param.22) | copy-start | bytes 393220
  19.7 5.7 %copy-start.26 = (bf16[512,128]{1,0:T(8,128)(2,1)S(1)}, bf16[512,128]{1,0:T(8,128)(2,1)}, u32[]{:S(2)}) copy-start(bf16[512,128]{1,0:T(8,128)(2,1)} %convolution_convert_fusion.4) | copy-start | bytes 393220
  25.4 4.7 %copy-start.8 = (bf16[32,16,4,32]{3,2,1,0:T(4,128)(2,1)}, bf16[32,16,4,32]{3,2,1,0:T(4,128)(2,1)S(1)}, u32[]{:S(2)}) copy-start(bf16[32,16,4,32]{3,2,1,0:T(4,128)(2,1)S(1)} %reshape.255) | copy-start | bytes 393220
  32.5 3.6 %copy-start.12 = (bf16[512,128]{1,0:T(8,128)(2,1)}, bf16[512,128]{1,0:T(8,128)(2,1)S(1)}, u32[]{:S(2)}) copy-start(bf16[512,128]{1,0:T(8,128)(2,1)S(1)} %convert_element_type.138) | copy-start | bytes 393220
  33.8 82.4 %all-reduce.9.cloned.1.call-start = ((), (), s32[]{:S(2)}) async-start(), calls=%async_computation.1 | async-start | bytes 2097152 | tf_op jit(solution)/shard_map/psum | solution.py:136
  35.0 5.7 %copy-start.5 = (bf16[1,16,4,2,4,512]{5,4,3,2,1,0:T(4,128)(2,1)}, bf16[1,16,4,2,4,512]{5,4,3,2,1,0:T(4,128)(2,1)S(1)}, u32[]{:S(2)}) copy-start(bf16[1,16,4,2,4,512]{5,4,3,2,1,0:T(4,128)(2,1)S(1)} %reshape.259) | copy-start | bytes 1572868
  35.0 37.7 %copy-start.37 = (f32[512]{0:T(512)S(1)}, f32[512]{0:T(512)}, u32[]{:S(2)}) copy-start(f32[512]{0:T(512)} %param.29) | copy-start | bytes 6148
  40.7 33.9 %copy-start.34 = (f32[512]{0:T(512)S(1)}, f32[512]{0:T(512)}, u32[]{:S(2)}) copy-start(f32[512]{0:T(512)} %param.32) | copy-start | bytes 6148
  40.7 33.9 %copy-start.38 = (f32[512]{0:T(512)S(1)}, f32[512]{0:T(512)}, u32[]{:S(2)}) copy-start(f32[512]{0:T(512)} %param.33) | copy-start | bytes 6148
  40.7 33.9 %copy-start.49 = (f32[512]{0:T(512)S(1)}, f32[512]{0:T(512)}, u32[]{:S(2)}) copy-start(f32[512]{0:T(512)} %param.35) | copy-start | bytes 6148
  74.3 3.0 copy-start.1
  79.6 61.1 %all-gather.3.cloned.1.call-start = ((), (), s32[]{:S(2)}) async-start(), calls=%async_computation.3 | async-start | bytes 2621440 | tf_op jit(solution)/shard_map/all_gather | solution.py:125
  82.2 116.6 %all-reduce.11.cloned.1.call-start = ((), (), s32[]{:S(2)}) async-start(), calls=%async_computation.2 | async-start | bytes 2097152 | tf_op jit(solution)/shard_map/psum | solution.py:171
  83.7 4.3 %copy-start.2 = (f32[512,512]{1,0:T(8,128)S(1)}, f32[512,512]{1,0:T(8,128)}, u32[]{:S(2)}) copy-start(f32[512,512]{1,0:T(8,128)} %copy-done.1) | copy-start | bytes 3145732
  85.0 3.0 copy-start.11
  89.7 53.9 %copy-start.39 = (f32[512]{0:T(512)S(1)}, f32[512]{0:T(512)}, u32[]{:S(2)}) copy-start(f32[512]{0:T(512)} %param.37) | copy-start | bytes 6148
  143.6 4.5 %copy-start.30 = (f32[32,4,16]{2,1,0:T(4,128)S(1)}, f32[32,4,16]{2,1,0:T(4,128)}, u32[]{:S(2)}) copy-start(f32[32,4,16]{2,1,0:T(4,128)} %copy-done.29) | copy-start | bytes 24580
  148.1 3.2 copy-start.14
  148.1 3.1 copy-start.20
  157.7 3.5 copy-start.25
  161.2 3.5 copy-start.4
  161.2 3.5 copy-start.13
  162.6 174.6 %all-reduce.13.cloned.1.call-start = ((), (), s32[]{:S(2)}) async-start(), calls=%async_computation.4 | async-start | bytes 6291456 | tf_op jit(solution)/shard_map/psum | solution.py:191
  169.2 4.9 %copy-start.46 = (s32[256]{0:T(256)S(1)}, s32[256]{0:T(256)}, u32[]{:S(2)}) copy-start(s32[256]{0:T(256)} %copy-done.45) | copy-start | bytes 3076
  169.2 29.6 %copy-start.32 = (f32[512]{0:T(512)S(1)}, f32[512]{0:T(512)}, u32[]{:S(2)}) copy-start(f32[512]{0:T(512)} %div.35) | copy-start | bytes 6148
  169.2 29.6 %copy-start.33 = (f32[512]{0:T(512)S(1)}, f32[512]{0:T(512)}, u32[]{:S(2)}) copy-start(f32[512]{0:T(512)} %rsqrt.21) | copy-start | bytes 6148
  337.2 6.8 %copy-start.16 = (f32[512,512]{1,0:T(8,128)S(1)}, f32[512,512]{1,0:T(8,128)}, u32[]{:S(2)}) copy-start(f32[512,512]{1,0:T(8,128)} %get-tuple-element.76) | copy-start | bytes 3145732
  337.2 7.8 %copy-start.15 = (f32[512,512]{1,0:T(8,128)S(1)}, f32[512,512]{1,0:T(8,128)}, u32[]{:S(2)}) copy-start(f32[512,512]{1,0:T(8,128)} %get-tuple-element.78) | copy-start | bytes 3145732
  (23 other events, 40.3 us)
Sparse Core Ops, SparseCore 0:
  33.9 38.8 all-reduce.6
  79.7 36.4 all-reduce.8
  117.7 22.9 all-gather.2
  162.7 36.0 all-reduce.10
  204.7 132.4 all-reduce.12
